TPU v7x, 512 devices: a whole 4x4x16 slice. The times are simulated.
512 devices in a mesh: dp: 32 (over z, y_lo), fsdp: 16 (over x, y_hi, core).
Axes of the slice: x: 4, y: 4 (y_hi: 2, y_lo: 2; y = y_hi * 2 + y_lo), z: 16, core: 2. Of those that a mesh axis runs over, the one named last changes fastest.
Arguments:
- tokens: bfloat16 [65536, 1024], P(('dp', 'fsdp')), may hold values from -6 to 6
- cotangent: bfloat16 [65536, 1024], P(('dp', 'fsdp')), may hold values from -6 to 6
- routes: int32 [65536, 1], P(('dp', 'fsdp')), may hold values from 0 to 32; in each aligned block of 128 rows (0 to 127, 128 to 255, ...) at most 4 rows name the same one
- norm_gain_vector: float32 [1024], replicated, may hold values from 0.25 to 1.75
- up_weight: bfloat16 [1024, 4096], P(None, 'fsdp'), may hold values from -0.1875 to 0.1875
- up_bias: float32 [4096], P('fsdp'), may hold values from -4 to 4
- down_weight: bfloat16 [4096, 1024], P('fsdp'), may hold values from -0.09375 to 0.09375
Outputs:
- input_grad: bfloat16 [65536, 1024], P(('dp', 'fsdp'))
- up_grad: float32 [1024, 4096], P(None, 'fsdp')
- bias_grad: float32 [4096], P('fsdp')
- down_grad: float32 [4096, 1024], P('fsdp')
- gain_grad: float32 [1024], replicated
Inputs may be any that keep to these rules, and one draw needn't show every extreme that they name: `routes`: among the 128 slots of one device no value below 32 appears more than 4 times; the value 32 marks a padding slot.
All inputs are finite; a program needn't handle non-finite values.
Results may differ from a plain program's by a relative error of at most 0.024.
Values may be sent and summed in bfloat16 or wider, within the bound.
A program may use at most 128 MiB of HBM per device.

v0:
```python
import jax
import jax.numpy as jnp
from jax import lax
from jax.sharding import Mesh
from jax.sharding import PartitionSpec as P

DP = ("dp_0", "dp_1")
FSDP = ("fsdp_0", "fsdp_1", "fsdp_2")
ROWS_AXES = ("fsdp_0", "fsdp_1")
DP_FSDP = ("dp_0", "dp_1", "fsdp_0", "fsdp_1", "fsdp_2")
root_two_pi = 0.7978845608
cubic = 0.044715


def side_by_side(arrays, axis, split_dim, concat_dim, along):
    both = jnp.concatenate(arrays, axis=along)
    filled, at, finished = (
        lax.all_to_all(both, axis, split_axis=split_dim, concat_axis=concat_dim, tiled=True),
        0,
        [],
    )
    for a in arrays:
        finished.append(lax.slice_in_dim(filled, at, at + a.shape[along], axis=along))
        at += a.shape[along]
    return tuple(finished)


def gelu_pair(pre):
    inner = root_two_pi * (pre + cubic * pre * pre * pre)
    tangent = jnp.tanh(inner)
    act = 0.5 * pre * (1.0 + tangent)
    slope = 0.5 * (1.0 + tangent) + 0.5 * pre * (1.0 - tangent * tangent) * root_two_pi * (
        1.0 + 3.0 * cubic * pre * pre
    )
    return (act, slope)


def apply_layer_norm(values):
    row_average = jnp.mean(values, axis=1, keepdims=True)
    centered = values - row_average
    variance = jnp.mean(centered * centered, axis=1, keepdims=True)
    inverse_std = 1.0 / jnp.sqrt(variance + 1e-05)
    return (centered * inverse_std, inverse_std)


def shards(tokens, cotangent, routes, norm_gain_vector, up_weight, up_bias, down_weight):
    particle_slot_count = tokens.shape[0]
    dp_size = lax.axis_size(DP)
    capacity = particle_slot_count // dp_size
    up_weight = lax.all_gather(up_weight, "fsdp_2", axis=1, tiled=True)
    down_weight = lax.all_gather(down_weight, "fsdp_2", axis=0, tiled=True)
    up_bias = lax.all_gather(up_bias, "fsdp_2", axis=0, tiled=True)
    target = routes[:, 0]
    matches = (target[:, None] == jnp.arange(dp_size + 1, dtype=jnp.int32)[None, :]).astype(
        jnp.int32
    )
    earlier = jnp.cumsum(matches, axis=0) - matches
    ranked = jnp.sum(earlier * matches, axis=1)
    slot_index = jnp.where(target < dp_size, target * capacity + ranked, -1)
    placing = (
        slot_index[None, :] == jnp.arange(particle_slot_count, dtype=jnp.int32)[:, None]
    ).astype(jnp.bfloat16)
    send_in = jnp.dot(placing, tokens, preferred_element_type=jnp.float32).astype(jnp.bfloat16)
    send_cot = jnp.dot(placing, cotangent, preferred_element_type=jnp.float32).astype(jnp.bfloat16)
    packed_in, packed_cot = side_by_side((send_in, send_cot), DP, 0, 0, 1)
    local_standardized, own_inverse = apply_layer_norm(packed_in.astype(jnp.float32))
    normed_local = (local_standardized * norm_gain_vector).astype(jnp.bfloat16)
    all_cot = lax.all_gather(packed_cot, ROWS_AXES, axis=0, tiled=True)
    gathered_normed_rows = lax.all_gather(normed_local, ROWS_AXES, axis=0, tiled=True)
    pre = jnp.dot(gathered_normed_rows, up_weight, preferred_element_type=jnp.float32) + up_bias
    act_full, slope = gelu_pair(pre)
    act = act_full.astype(jnp.bfloat16)
    act_grad = jnp.einsum("rd,kd->rk", all_cot, down_weight, preferred_element_type=jnp.float32)
    pre_grad = (act_grad * slope).astype(jnp.bfloat16)
    down_part = jnp.einsum("rk,rd->kd", act, all_cot, preferred_element_type=jnp.float32)
    up_part = jnp.einsum(
        "rk,rd->kd", pre_grad, gathered_normed_rows, preferred_element_type=jnp.float32
    )
    bias_part = jnp.sum(pre_grad.astype(jnp.float32), axis=0)
    partial_gain_grad = (
        jnp.sum(up_part * up_weight.T.astype(jnp.float32), axis=0) / norm_gain_vector
    )
    parts = jnp.concatenate([up_part, down_part], axis=1).astype(jnp.bfloat16)
    mine = lax.psum_scatter(parts, "fsdp_2", scatter_dimension=0, tiled=True)
    mine = lax.psum_scatter(mine, DP, scatter_dimension=0, tiled=True)
    whole = lax.all_gather(mine, DP, axis=0, tiled=True).astype(jnp.float32)
    d = up_weight.shape[0]
    up_grad = whole[:, :d].T
    down_grad = whole[:, d:]
    normed_rows_gradient = lax.psum_scatter(
        jnp.einsum("rk,dk->rd", pre_grad, up_weight, preferred_element_type=jnp.float32).astype(
            jnp.bfloat16
        ),
        ROWS_AXES,
        scatter_dimension=0,
        tiled=True,
    ).astype(jnp.float32)
    index = lax.axis_index(FSDP)
    k = bias_part.shape[0] // 2
    wide = jnp.zeros((8, 2 * k), jnp.float32)
    wide = lax.dynamic_update_slice(wide, bias_part[None], (index // 2, 0))
    small = lax.psum(jnp.concatenate([partial_gain_grad, wide.reshape(-1)]), DP_FSDP)
    gain_grad = small[:d]
    bias_grad = lax.dynamic_slice(small[d:], (index * k,), (k,))
    scaled_values = normed_rows_gradient * norm_gain_vector
    final_result = packed_cot.astype(jnp.float32) + own_inverse * (
        scaled_values
        - jnp.mean(scaled_values, axis=1, keepdims=True)
        - local_standardized * jnp.mean(scaled_values * local_standardized, axis=1, keepdims=True)
    )
    return (final_result.astype(jnp.bfloat16), up_grad, bias_grad, down_grad, gain_grad)


def solution(mesh):
    finer = Mesh(
        mesh.devices.reshape(16, 2, 4, 2, 2), ("dp_0", "dp_1", "fsdp_0", "fsdp_1", "fsdp_2")
    )
    return jax.shard_map(
        shards,
        mesh=finer,
        in_specs=(
            P(DP_FSDP, None),
            P(DP_FSDP, None),
            P(DP_FSDP, None),
            P(),
            P(None, FSDP),
            P(FSDP),
            P(FSDP, None),
        ),
        out_specs=(P(DP_FSDP, None), P(None, FSDP), P(FSDP), P(FSDP, None), P()),
        check_vma=False,
    )
```

profile of v0, /device:TPU:2, one launch (start us, length us, event | category | flops | bytes accessed | tf_op | source)
XLA Modules:
  0.0 631.0 jit_solution(15258363506738329338)
XLA Ops:
  7.2 0.8 fusion.26
  8.0 0.2 reduce_window_sum.11
  8.1 0.8 select_reduce_fusion
  9.0 0.7 compare_select_fusion
  9.6 0.2 convolution_convert_fusion.2
  9.9 1.2 convolution_convert_fusion.3
  11.1 1.0 all_to_all.8
  12.1 16.6 %all-to-all-start = ((bf16[32,4,2048]{2,1,0:T(4,128)(2,1)}), bf16[32,4,2048]{2,1,0:T(4,128)(2,1)S(1)}, u32[]{:S(2)}, u32[]{:S(2)}) async-start(bf16[32,4,2048]{2,1,0:T(4,128)(2,1)} %all_to_all.8), calls=%async_computation | async-start | bytes 1048576 | tf_op jit(solution)/shard_map/all_to_all | solution.py:18
  28.7 0.0 all-gather.13.cloned.1.call-start
  28.8 1.0 copy.14
  29.8 0.0 all-gather.13.cloned.1.call-update
  29.8 0.0 all-gather.11.cloned.1.call-start
  29.9 31.9 %all-to-all-done = bf16[32,4,2048]{2,1,0:T(4,128)(2,1)S(1)} async-done(((bf16[32,4,2048]{2,1,0:T(4,128)(2,1)}), bf16[32,4,2048]{2,1,0:T(4,128)(2,1)S(1)}, u32[]{:S(2)}, u32[]{:S(2)}) %all-to-all-start) | async-done | bytes 524320 | tf_op jit(solution)/shard_map/all_to_all | solution.py:18
  61.7 0.1 all_to_all.10
  61.9 0.1 convert_reduce_fusion.1
  62.0 0.2 fusion.24
  62.2 0.9 fusion.18
  63.2 0.0 all-gather.7.cloned.1.call-start
  63.2 0.7 slice.24
  64.0 0.0 all-gather.9.cloned.1.call-start
  64.0 0.5 all-gather.9.cloned.1.call-update
  64.5 0.0 reduce-scatter.6.cloned.1.call-start
  64.6 1.8 all-gather
  66.4 61.5 %all-gather.11.cloned.1.call-done = bf16[1024,1024]{1,0:T(8,128)(2,1)} async-done(((bf16[128,1024]{1,0:T(8,128)(2,1)}), bf16[1024,1024]{1,0:T(8,128)(2,1)}) %all-gather.11.cloned.1.call-update) | async-done | bytes 2097168 | tf_op jit(solution)/shard_map/all_gather | solution.py:69
  127.9 4.4 fusion.33
  132.4 68.8 %all-gather.7.cloned.1.call-done = bf16[1024,1024]{1,0:T(8,128)(2,1)} async-done(((bf16[128,1024]{1,0:T(8,128)(2,1)}), bf16[1024,1024]{1,0:T(8,128)(2,1)}) %all-gather.7.cloned.1.call-update) | async-done | bytes 2097168 | tf_op jit(solution)/shard_map/all_gather | solution.py:68
  201.1 3.6 convolution_convert_fusion.1
  204.8 17.0 %all-gather.9.cloned.1.call-done = bf16[512,1024]{1,0:T(8,128)(2,1)} async-done(((bf16[256,1024]{1,0:T(8,128)(2,1)}), bf16[512,1024]{1,0:T(8,128)(2,1)}) %all-gather.9.cloned.1.call-update) | async-done | bytes 1048592 | tf_op jit(solution)/shard_map/all_gather | solution.py:51
  221.8 5.1 convert_reduce_fusion
  226.9 1.3 fusion.7
  228.2 1.5 pad_maximum_fusion
  229.7 0.0 reduce-scatter.8.cloned.1.call-start
  229.8 21.8 %reduce-scatter.6.cloned.1.call-done = bf16[256,2048]{1,0:T(8,128)(2,1)} async-done(((bf16[512,2048]{1,0:T(8,128)(2,1)}), bf16[256,2048]{1,0:T(8,128)(2,1)}) %reduce-scatter.6.cloned.1.call-update) | async-done | bytes 1048592 | tf_op jit(solution)/shard_map/reduce_scatter | solution.py:84
  251.6 0.0 reduce-scatter.4.cloned.1.call-start
  251.6 2.6 convolution_convert_fusion
  254.3 0.0 all-gather.15.cloned.1.call-start
  254.3 139.2 %reduce-scatter.8.cloned.1.call-done = bf16[8,2048]{1,0:T(8,128)(2,1)} async-done(((bf16[256,2048]{1,0:T(8,128)(2,1)}), bf16[8,2048]{1,0:T(8,128)(2,1)}) %reduce-scatter.8.cloned.1.call-update) | async-done | bytes 32784 | tf_op jit(solution)/shard_map/reduce_scatter | solution.py:85
  393.6 0.1 dynamic_update_slice.3
  393.7 100.6 %psum.7 = f32[5120]{0:T(1024)S(1)} all-reduce(f32[5120]{0:T(1024)S(1)} %pad_maximum_fusion.2), channel_id=1, replica_groups=mesh['dp_0'=16,'dp_1'=2,'fsdp_0'=4,'fsdp_1'=2,'fsdp_2'=2] {'dp_0','dp_1'..., use_global_device_ids=true, to_apply=%region_11.12 | all-reduce | flops 5120 | bytes 40960 | tf_op jit(solution)/shard_map/psum | solution.py:102
  494.2 0.6 slice.29
  494.8 0.6 dynamic_slice.3
  495.5 1.2 fusion.25
  496.7 1.9 fusion.23
  498.6 121.5 %all-gather.15.cloned.1.call-done = bf16[256,2048]{1,0:T(8,128)(2,1)} async-done(((bf16[8,2048]{1,0:T(8,128)(2,1)}), bf16[256,2048]{1,0:T(8,128)(2,1)}) %all-gather.15.cloned.1.call-update) | async-done | bytes 1048592 | tf_op jit(solution)/shard_map/all_gather | solution.py:86
  620.1 1.5 convert_element_type.58
  621.6 0.1 slice_bitcast_fusion
  621.7 1.3 copy.15
  623.0 1.1 slice.28
  (35 shorter events, 0.2 us)
Async XLA Ops:
  7.2 2.5 copy-start
  9.6 19.1 %copy-start.2 = (bf16[1024,256]{1,0:T(8,128)(2,1)S(1)}, bf16[1024,256]{1,0:T(8,128)(2,1)}, u32[]{:S(2)}) copy-start(bf16[1024,256]{1,0:T(8,128)(2,1)} %param.11) | copy-start | bytes 1572868
  12.1 50.1 %copy-start.3 = (f32[1024]{0:T(1024)S(1)}, f32[1024]{0:T(1024)}, u32[]{:S(2)}) copy-start(f32[1024]{0:T(1024)} %param.10) | copy-start | bytes 12292
  12.1 49.7 %all-to-all-start = ((bf16[32,4,2048]{2,1,0:T(4,128)(2,1)}), bf16[32,4,2048]{2,1,0:T(4,128)(2,1)S(1)}, u32[]{:S(2)}, u32[]{:S(2)}) async-start(bf16[32,4,2048]{2,1,0:T(4,128)(2,1)} %all_to_all.8), calls=%async_computation | async-start | bytes 1048576 | tf_op jit(solution)/shard_map/all_to_all | solution.py:18
  28.7 37.7 %all-gather.13.cloned.1.call-start = ((), (), s32[]{:S(2)}) async-start(), calls=%async_computation.7 | async-start | bytes 1572864 | tf_op jit(solution)/shard_map/all_gather | solution.py:50
  29.8 34.8 %copy-start.4 = (f32[256]{0:T(256)S(1)}, f32[256]{0:T(256)}, u32[]{:S(2)}) copy-start(f32[256]{0:T(256)} %param.12) | copy-start | bytes 3076
  29.8 98.1 %all-gather.11.cloned.1.call-start = ((), (), s32[]{:S(2)}) async-start(), calls=%async_computation.6 | async-start | bytes 2359296 | tf_op jit(solution)/shard_map/all_gather | solution.py:69
  63.2 138.0 %all-gather.7.cloned.1.call-start = ((), (), s32[]{:S(2)}) async-start(), calls=%async_computation.4 | async-start | bytes 2359296 | tf_op jit(solution)/shard_map/all_gather | solution.py:68
  64.0 157.8 %all-gather.9.cloned.1.call-start = ((), (), s32[]{:S(2)}) async-start(), calls=%async_computation.5 | async-start | bytes 1572864 | tf_op jit(solution)/shard_map/all_gather | solution.py:51
  64.5 187.0 %reduce-scatter.6.cloned.1.call-start = ((), (), s32[]{:S(2)}) async-start(), calls=%async_computation.9 | async-start | bytes 3145728 | tf_op jit(solution)/shard_map/reduce_scatter | solution.py:84
  204.7 22.2 %copy-start.6 = (bf16[1024,512]{0,1:T(8,128)(2,1)S(1)}, bf16[1024,512]{0,1:T(8,128)(2,1)}, u32[]{:S(2)}) copy-start(bf16[1024,512]{0,1:T(8,128)(2,1)} %all-gather.13.cloned.1.call-done) | copy-start | bytes 3145732
  221.8 5.1 copy-start.5
  226.9 1.3 copy-start.7
  229.7 21.9 %copy-start.8 = (bf16[1024,512]{1,0:T(8,128)(2,1)S(1)}, bf16[1024,512]{1,0:T(8,128)(2,1)}, u32[]{:S(2)}) copy-start(bf16[1024,512]{1,0:T(8,128)(2,1)} %copy-done.7) | copy-start | bytes 3145732
  229.7 163.8 %reduce-scatter.8.cloned.1.call-start = ((), (), s32[]{:S(2)}) async-start(), calls=%async_computation.10 | async-start | bytes 1081344 | tf_op jit(solution)/shard_map/reduce_scatter | solution.py:85
  251.6 243.9 %reduce-scatter.4.cloned.1.call-start = ((), (), s32[]{:S(2)}) async-start(), calls=%async_computation.8 | async-start | bytes 2359296 | tf_op jit(solution)/shard_map/reduce_scatter | solution.py:90
  254.3 365.9 %all-gather.15.cloned.1.call-start = ((), (), s32[]{:S(2)}) async-start(), calls=%async_computation.11 | async-start | bytes 1081344 | tf_op jit(solution)/shard_map/all_gather | solution.py:86
  621.6 1.4 copy-start.1
Sparse Core Ops, SparseCore 0:
  32.2 20.3 all-gather.12
  63.3 64.5 all-gather.10
  131.7 69.3 all-gather.6
  203.1 18.6 all-gather.8
  229.9 21.6 reduce-scatter.5
  254.2 139.2 reduce-scatter.7
  398.2 89.2 reduce-scatter.3
  489.5 130.5 all-gather.14
where the time goes:
time: 631 us
  waiting for transfers between devices  462 us (73%)
  blocking collectives  102 us (16%)
  matrix products  18.4 us (3%)
  starting transfers between devices  17 us (3%)
  between operations  14.4 us (2%)
  other arithmetic  9.85 us (2%)
  local copies, waits for them, and re-layouts  6.69 us (1%)
    reduce_scatter x1, waiting for transfers between devices, shards(): mine = lax.psum_scatter(mine, DP, scatter_dimension=0, tiled=True)  139 us
    all_gather x1, waiting for transfers between devices, shards(): whole = lax.all_gather(mine, DP, axis=0, tiled=True).astype(jnp.float32)  122 us
    psum x1, blocking collectives, shards(): lax.psum(jnp.concatenate([partial_gain_grad, wide.reshape(-1)]), DP_FSDP)  101 us
    all_gather x1, waiting for transfers between devices, shards(): all_cot = lax.all_gather(packed_cot, ROWS_AXES, axis=0, tiled=True)  68.8 us
    all_gather x1, waiting for transfers between devices, shards(): lax.all_gather(normed_local, ROWS_AXES, axis=0, tiled=True)  61.5 us
    all_to_all x1, waiting for transfers between devices, side_by_side(): lax.all_to_all(both, axis, split_axis=split_dim, concat_axis=concat_dim,...  31.9 us
    reduce_scatter x1, waiting for transfers between devices, shards(): mine = lax.psum_scatter(parts, 'fsdp_2', scatter_dimension=0, tiled=True)  21.8 us
    all_gather x1, waiting for transfers between devices, shards(): down_weight = lax.all_gather(down_weight, 'fsdp_2', axis=0, tiled=True)  17 us
  transfers between devices with their start and end apart: 9, of which 7 were waited for; matrix products, arithmetic and copies ran while one was open for 3% of the time, Pallas kernels for 0%

commit v1 on v0

--- a/solution.py
+++ b/solution.py
@@ -99,7 +99,9 @@
     k = bias_part.shape[0] // 2
     wide = jnp.zeros((8, 2 * k), jnp.float32)
     wide = lax.dynamic_update_slice(wide, bias_part[None], (index // 2, 0))
-    small = lax.psum(jnp.concatenate([partial_gain_grad, wide.reshape(-1)]), DP_FSDP)
+    small = jnp.sum(
+        lax.all_gather(jnp.concatenate([partial_gain_grad, wide.reshape(-1)]), DP_FSDP), axis=0
+    )
     gain_grad = small[:d]
     bias_grad = lax.dynamic_slice(small[d:], (index * k,), (k,))
     scaled_values = normed_rows_gradient * norm_gain_vector

time: 631 us -> 1480 us (2.35)
  the two profiles are of different devices: /device:TPU:2 before, /device:TPU:64 now
where the time goes in v1:
time: 1480 us
  waiting for transfers between devices  1390 us (94%)
  local copies, waits for them, and re-layouts  18.5 us (1%)
  matrix products  18.5 us (1%)
  starting transfers between devices  16.4 us (1%)
  other arithmetic  15 us (1%)
    all_gather x1, waiting for transfers between devices, shards(): lax.all_gather(jnp.concatenate([partial_gain_grad, wide.reshape(-1)]), DP...  832 us
    reduce_scatter x1, waiting for transfers between devices, shards(): mine = lax.psum_scatter(mine, DP, scatter_dimension=0, tiled=True)  135 us
    all_gather x1, waiting for transfers between devices, shards(): whole = lax.all_gather(mine, DP, axis=0, tiled=True).astype(jnp.float32)  127 us
    reduce_scatter x1, waiting for transfers between devices, shards(): lax.psum_scatter(jnp.einsum('rk,dk->rd', pre_grad, up_weight, preferred_e...  97.9 us
    all_gather x1, waiting for transfers between devices, shards(): all_cot = lax.all_gather(packed_cot, ROWS_AXES, axis=0, tiled=True)  68.8 us
    all_gather x1, waiting for transfers between devices, shards(): lax.all_gather(normed_local, ROWS_AXES, axis=0, tiled=True)  66 us
  transfers between devices with their start and end apart: 10, of which 9 were waited for; matrix products, arithmetic and copies ran while one was open for 1% of the time, Pallas kernels for 0%

profile of v1, /device:TPU:64, one launch (start us, length us, event | category | flops | bytes accessed | tf_op | source)
XLA Modules:
  0.0 1478.0 jit_solution(10748626825134161292)
XLA Ops:
  7.2 0.8 fusion.26
  8.0 0.2 reduce_window_sum.11
  8.1 0.8 select_reduce_fusion
  9.0 0.7 compare_select_fusion
  9.6 0.2 convolution_convert_fusion.2
  9.9 1.2 convolution_convert_fusion.3
  11.1 1.0 all_to_all.8
  12.1 16.0 %all-to-all-start = ((bf16[32,4,2048]{2,1,0:T(4,128)(2,1)}), bf16[32,4,2048]{2,1,0:T(4,128)(2,1)S(1)}, u32[]{:S(2)}, u32[]{:S(2)}) async-start(bf16[32,4,2048]{2,1,0:T(4,128)(2,1)} %all_to_all.8), calls=%async_computation | async-start | bytes 1048576 | tf_op jit(solution)/shard_map/all_to_all | solution.py:18
  28.1 0.0 all-gather.15.cloned.1.call-start
  28.2 1.0 copy.16
  29.2 0.0 all-gather.13.cloned.1.call-start
  29.3 27.6 %all-to-all-done = bf16[32,4,2048]{2,1,0:T(4,128)(2,1)S(1)} async-done(((bf16[32,4,2048]{2,1,0:T(4,128)(2,1)}), bf16[32,4,2048]{2,1,0:T(4,128)(2,1)S(1)}, u32[]{:S(2)}, u32[]{:S(2)}) %all-to-all-start) | async-done | bytes 524320 | tf_op jit(solution)/shard_map/all_to_all | solution.py:18
  56.9 0.1 all_to_all.10
  57.0 0.1 convert_reduce_fusion.1
  57.1 0.2 fusion.24
  57.3 0.9 fusion.18
  58.3 0.0 all-gather.9.cloned.1.call-start
  58.4 0.7 slice.24
  59.1 0.0 all-gather.11.cloned.1.call-start
  59.1 0.5 all-gather.11.cloned.1.call-update
  59.7 1.8 all-gather.1
  61.5 66.0 %all-gather.13.cloned.1.call-done = bf16[1024,1024]{1,0:T(8,128)(2,1)} async-done(((bf16[128,1024]{1,0:T(8,128)(2,1)}), bf16[1024,1024]{1,0:T(8,128)(2,1)}) %all-gather.13.cloned.1.call-update) | async-done | bytes 2097168 | tf_op jit(solution)/shard_map/all_gather | solution.py:69
  127.5 4.5 fusion.33
  132.0 68.8 %all-gather.9.cloned.1.call-done = bf16[1024,1024]{1,0:T(8,128)(2,1)} async-done(((bf16[128,1024]{1,0:T(8,128)(2,1)}), bf16[1024,1024]{1,0:T(8,128)(2,1)}) %all-gather.9.cloned.1.call-update) | async-done | bytes 2097168 | tf_op jit(solution)/shard_map/all_gather | solution.py:68
  200.7 3.6 convolution_convert_fusion.1
  204.4 16.7 %all-gather.11.cloned.1.call-done = bf16[512,1024]{1,0:T(8,128)(2,1)} async-done(((bf16[256,1024]{1,0:T(8,128)(2,1)}), bf16[512,1024]{1,0:T(8,128)(2,1)}) %all-gather.11.cloned.1.call-update) | async-done | bytes 1048592 | tf_op jit(solution)/shard_map/all_gather | solution.py:51
  221.1 5.1 convert_reduce_fusion
  226.2 1.3 fusion.7
  227.5 1.5 pad_maximum_fusion
  229.1 21.8 %reduce-scatter.6.cloned.1.call-done = bf16[256,2048]{1,0:T(8,128)(2,1)} async-done(((bf16[512,2048]{1,0:T(8,128)(2,1)}), bf16[256,2048]{1,0:T(8,128)(2,1)}) %reduce-scatter.6.cloned.1.call-update) | async-done | bytes 1048592 | tf_op jit(solution)/shard_map/reduce_scatter | solution.py:84
  251.0 2.6 convolution_convert_fusion
  253.6 0.0 all-gather.17.cloned.1.call-start
  253.7 134.8 %reduce-scatter.8.cloned.1.call-done = bf16[8,2048]{1,0:T(8,128)(2,1)} async-done(((bf16[256,2048]{1,0:T(8,128)(2,1)}), bf16[8,2048]{1,0:T(8,128)(2,1)}) %reduce-scatter.8.cloned.1.call-update) | async-done | bytes 32784 | tf_op jit(solution)/shard_map/reduce_scatter | solution.py:85
  388.5 0.1 dynamic_update_slice.3
  388.6 0.6 pad_maximum_fusion.2
  389.3 97.9 %reduce-scatter.4.cloned.1.call-done = bf16[128,1024]{1,0:T(8,128)(2,1)} async-done(((bf16[1024,1024]{1,0:T(8,128)(2,1)}), bf16[128,1024]{1,0:T(8,128)(2,1)}) %reduce-scatter.4.cloned.1.call-update) | async-done | bytes 262160 | tf_op jit(solution)/shard_map/reduce_scatter | solution.py:90
  487.2 1.2 fusion.25
  488.3 1.9 fusion.23
  490.3 127.4 %all-gather.17.cloned.1.call-done = bf16[256,2048]{1,0:T(8,128)(2,1)} async-done(((bf16[8,2048]{1,0:T(8,128)(2,1)}), bf16[256,2048]{1,0:T(8,128)(2,1)}) %all-gather.17.cloned.1.call-update) | async-done | bytes 1048592 | tf_op jit(solution)/shard_map/all_gather | solution.py:86
  617.6 1.5 convert_element_type.58
  619.1 0.1 slice_bitcast_fusion
  619.2 1.3 copy.17
  620.5 1.1 slice.28
  621.6 832.3 %all-gather.19.cloned.1.call-done = f32[2621440]{0:T(1024)} async-done(((f32[5120]{0:T(1024)}), f32[2621440]{0:T(1024)}) %all-gather.19.cloned.1.call-update) | async-done | bytes 10485776 | tf_op jit(solution)/shard_map/all_gather | solution.py:103
  1453.9 11.8 reshape.52
  1465.7 4.5 reduce_sum.79
  1470.2 0.6 slice.29
  1470.8 0.6 dynamic_slice.3
  (39 shorter events, 0.4 us)
Async XLA Ops:
  7.2 2.5 copy-start
  9.6 18.5 %copy-start.2 = (bf16[1024,256]{1,0:T(8,128)(2,1)S(1)}, bf16[1024,256]{1,0:T(8,128)(2,1)}, u32[]{:S(2)}) copy-start(bf16[1024,256]{1,0:T(8,128)(2,1)} %param.11) | copy-start | bytes 1572868
  12.1 45.3 %copy-start.3 = (f32[1024]{0:T(1024)S(1)}, f32[1024]{0:T(1024)}, u32[]{:S(2)}) copy-start(f32[1024]{0:T(1024)} %param.10) | copy-start | bytes 12292
  12.1 44.8 %all-to-all-start = ((bf16[32,4,2048]{2,1,0:T(4,128)(2,1)}), bf16[32,4,2048]{2,1,0:T(4,128)(2,1)S(1)}, u32[]{:S(2)}, u32[]{:S(2)}) async-start(bf16[32,4,2048]{2,1,0:T(4,128)(2,1)} %all_to_all.8), calls=%async_computation | async-start | bytes 1048576 | tf_op jit(solution)/shard_map/all_to_all | solution.py:18
  28.1 33.4 %all-gather.15.cloned.1.call-start = ((), (), s32[]{:S(2)}) async-start(), calls=%async_computation.7 | async-start | bytes 1572864 | tf_op jit(solution)/shard_map/all_gather | solution.py:50
  29.2 30.5 %copy-start.4 = (f32[256]{0:T(256)S(1)}, f32[256]{0:T(256)}, u32[]{:S(2)}) copy-start(f32[256]{0:T(256)} %param.12) | copy-start | bytes 3076
  29.2 98.3 %all-gather.13.cloned.1.call-start = ((), (), s32[]{:S(2)}) async-start(), calls=%async_computation.6 | async-start | bytes 2359296 | tf_op jit(solution)/shard_map/all_gather | solution.py:69
  58.3 142.4 %all-gather.9.cloned.1.call-start = ((), (), s32[]{:S(2)}) async-start(), calls=%async_computation.4 | async-start | bytes 2359296 | tf_op jit(solution)/shard_map/all_gather | solution.py:68
  59.1 162.0 %all-gather.11.cloned.1.call-start = ((), (), s32[]{:S(2)}) async-start(), calls=%async_computation.5 | async-start | bytes 1572864 | tf_op jit(solution)/shard_map/all_gather | solution.py:51
  59.7 191.2 %reduce-scatter.6.cloned.1.call-start = ((), (), s32[]{:S(2)}) async-start(), calls=%async_computation.9 | async-start | bytes 3145728 | tf_op jit(solution)/shard_map/reduce_scatter | solution.py:84
  204.3 21.9 %copy-start.6 = (bf16[1024,512]{0,1:T(8,128)(2,1)S(1)}, bf16[1024,512]{0,1:T(8,128)(2,1)}, u32[]{:S(2)}) copy-start(bf16[1024,512]{0,1:T(8,128)(2,1)} %all-gather.15.cloned.1.call-done) | copy-start | bytes 3145732
  221.1 5.1 copy-start.5
  226.2 1.3 copy-start.7
  229.1 21.9 %copy-start.8 = (bf16[1024,512]{1,0:T(8,128)(2,1)S(1)}, bf16[1024,512]{1,0:T(8,128)(2,1)}, u32[]{:S(2)}) copy-start(bf16[1024,512]{1,0:T(8,128)(2,1)} %copy-done.7) | copy-start | bytes 3145732
  229.1 159.4 %reduce-scatter.8.cloned.1.call-start = ((), (), s32[]{:S(2)}) async-start(), calls=%async_computation.10 | async-start | bytes 1081344 | tf_op jit(solution)/shard_map/reduce_scatter | solution.py:85
  250.9 236.2 %reduce-scatter.4.cloned.1.call-start = ((), (), s32[]{:S(2)}) async-start(), calls=%async_computation.8 | async-start | bytes 2359296 | tf_op jit(solution)/shard_map/reduce_scatter | solution.py:90
  253.6 364.0 %all-gather.17.cloned.1.call-start = ((), (), s32[]{:S(2)}) async-start(), calls=%async_computation.11 | async-start | bytes 1081344 | tf_op jit(solution)/shard_map/all_gather | solution.py:86
  388.5 1065.5 %all-gather.19.cloned.1.call-start = ((), (), s32[]{:S(2)}) async-start(), calls=%async_computation.12 | async-start | bytes 10506240 | tf_op jit(solution)/shard_map/all_gather | solution.py:103
  619.1 1.4 copy-start.1
Sparse Core Ops, SparseCore 0:
  31.6 20.2 all-gather.14
  58.4 69.0 all-gather.12
  131.3 69.3 all-gather.8
  202.7 18.3 all-gather.10
  229.2 21.6 reduce-scatter.5
  253.5 134.8 reduce-scatter.7
  393.1 94.0 reduce-scatter.3
  489.2 128.3 all-gather.16
  619.9 834.0 all-gather.18
